TPU v7x, 32 devices: a whole 2x2x4 slice. The times are simulated.
32 devices in a mesh: dp: 4 (over y, core), tensor: 8 (over z, x).
Axes of the slice: x: 2, y: 2, z: 4, core: 2. Of those that a mesh axis runs over, the one named last changes fastest.
Arguments:
- inputs: bfloat16 [8192, 1024], P(('dp', 'tensor')), may hold values from -6 to 6
- qkv_weight: bfloat16 [1024, 3072], P(None, 'tensor'), may hold values from -0.1875 to 0.1875
- qkv_bias: bfloat16 [3072], P('tensor'), may hold values from -3 to 3
- dense_weight: bfloat16 [1024, 1024], P('tensor'), may hold values from -1 to 1
- up_weight: bfloat16 [1024, 4096], P(None, 'tensor'), may hold values from -0.1875 to 0.1875
- up_bias: bfloat16 [4096], P('tensor'), may hold values from -3 to 3
- down_weight: bfloat16 [4096, 1024], P('tensor'), may hold values from -0.09375 to 0.09375
- out_bias: bfloat16 [1024], replicated, may hold values from -3 to 3
- gain_one: bfloat16 [1024], replicated, may hold values from 0.099609375 to 1.8984375
- shift_one: bfloat16 [1024], replicated, may hold values from -2 to 2
- gain_two: bfloat16 [1024], replicated, may hold values from 0.099609375 to 1.8984375
- shift_two: bfloat16 [1024], replicated, may hold values from -2 to 2
- feature_omega: float32 [64, 64], replicated, may hold values from -0.75 to 0.75
- doc_ids: int32 [4, 2048], P('dp'), may hold values from 0 to 7, never falling along the last dimension, each value on 1 to 1024 neighbouring positions
- out_grad: bfloat16 [8192, 1024], P(('dp', 'tensor')), may hold values from -6 to 6
Outputs:
- layer_out: bfloat16 [8192, 1024], P(('dp', 'tensor'))
- input_grad: float32 [8192, 1024], P(('dp', 'tensor'))
- qkv_weight_grad: float32 [1024, 3072], P(None, 'tensor')
- qkv_bias_grad: float32 [3072], P('tensor')
- dense_weight_grad: float32 [1024, 1024], P('tensor')
- up_weight_grad: float32 [1024, 4096], P(None, 'tensor')
- up_bias_grad: float32 [4096], P('tensor')
- down_weight_grad: float32 [4096, 1024], P('tensor')
- out_bias_grad: float32 [1024], P('tensor')
- gain_one_grad: float32 [1024], P('tensor')
- shift_one_grad: float32 [1024], P('tensor')
- gain_two_grad: float32 [1024], P('tensor')
- shift_two_grad: float32 [1024], P('tensor')
Inputs may be any that keep to these rules, and one draw needn't show every extreme that they name: `doc_ids`: in each packed row the document numbers never fall; a document holds at most 1024 tokens and some document holds exactly that many.
All inputs are finite; a program needn't handle non-finite values.
Results may differ from a plain program's by a relative error of at most 0.0072.
Values may be sent and summed in bfloat16 or wider, within the bound.
No kernel may reach another device: no remote copies, remote signals or barrier semaphores. Data moves between devices by JAX's collectives and lax.ppermute only.
A program may use at most 192 MiB of HBM per device.

v0:
```python
import jax
import jax.numpy as jnp
from jax import lax
from jax.sharding import PartitionSpec as P

HEAD_DIM = 64
ROT = 16
LEN = 2048
EPS = 1e-05
EXACT = lax.Precision.HIGHEST


def layer_norm(values, gain_row, offset):
    row_mean = jnp.mean(values, axis=-1, keepdims=True)
    centred = values - row_mean
    spread = jnp.mean(centred * centred, axis=-1, keepdims=True)
    return centred * lax.rsqrt(spread + EPS) * gain_row + offset


def both_norms(token_rows, first_gain, first_offset, second_gain, second_offset):
    return (
        layer_norm(token_rows, first_gain, first_offset),
        layer_norm(token_rows, second_gain, second_offset),
    )


def exact_gelu(values):
    return jax.nn.gelu(values, approximate=False)


def dct_matrix(extent):
    indices = jnp.arange(extent, dtype=jnp.float32)
    cosines = jnp.cos(jnp.pi * (indices[:, None] + 0.5) * indices[None, :] / extent)
    scales = jnp.where(indices == 0, jnp.sqrt(1.0 / extent), jnp.sqrt(2.0 / extent))
    return cosines * scales[None, :]


def rotary_tables(positions, turned):
    half_rot = turned // 2
    frequencies = 10000.0 ** (-(jnp.arange(half_rot, dtype=jnp.float32) * 2.0 / turned))
    angles = positions.astype(jnp.float32)[:, None] * frequencies[None, :]
    return (jnp.cos(angles), jnp.sin(angles))


def rotate(values, cosine_table, sine_table):
    half_rot = cosine_table.shape[-1]
    leading = values[..., :half_rot]
    trailing = values[..., half_rot : 2 * half_rot]
    return jnp.concatenate(
        [
            leading * cosine_table - trailing * sine_table,
            trailing * cosine_table + leading * sine_table,
            values[..., 2 * half_rot :],
        ],
        axis=-1,
    )


def feature_map(values, cosine_table, sine_table, mixing):
    return jnp.exp(jnp.dot(rotate(values, cosine_table, sine_table), mixing, precision=EXACT))


def to_blocks(values, sequences, block_rows):
    shaped = values.reshape(
        (sequences, values.shape[0] // (sequences * block_rows), block_rows) + values.shape[1:]
    )
    return jnp.swapaxes(shaped, 0, 1)


def from_blocks(values):
    joined = jnp.swapaxes(values, 0, 1)
    return joined.reshape((-1,) + joined.shape[3:])


def allowed_pairs(doc_block):
    block_width = doc_block.shape[-1]
    places = jnp.arange(block_width)
    causal = places[:, None] >= places[None, :]
    return (doc_block[:, :, None] == doc_block[:, None, :]) & causal[None]


def attend_forward(query_blocks, key_blocks, value_blocks, doc_blocks, before_docs):
    sequences = query_blocks.shape[1]
    features = query_blocks.shape[-1]
    initial = (
        jnp.zeros((sequences, features, value_blocks.shape[-1]), jnp.float32),
        jnp.zeros((sequences, features), jnp.float32),
    )

    def advance(running, pieces):
        memory, totals = running
        query_rows, key_rows, value_rows, doc_block, before_doc = pieces
        query_wide = query_rows.astype(jnp.float32)
        value_wide = value_rows.astype(jnp.float32)
        weights = jnp.where(
            allowed_pairs(doc_block),
            jnp.einsum("sbf,scf->sbc", query_rows, key_rows, preferred_element_type=jnp.float32),
            0.0,
        )
        carried = (doc_block == before_doc[:, None]).astype(jnp.float32)[:, :, None]
        numerator = jnp.einsum(
            "sbc,sce->sbe", weights, value_wide, precision=EXACT
        ) + carried * jnp.einsum("sbf,sfe->sbe", query_wide, memory, precision=EXACT)
        denominator = (
            jnp.sum(weights, axis=-1, keepdims=True)
            + carried * jnp.einsum("sbf,sf->sb", query_wide, totals, precision=EXACT)[:, :, None]
        )
        last_doc = doc_block[:, -1]
        retained = (last_doc == before_doc).astype(jnp.float32)
        chosen = key_rows * (doc_block == last_doc[:, None]).astype(jnp.bfloat16)[:, :, None]
        new_memory = retained[:, None, None] * memory + jnp.einsum(
            "sbf,sbe->sfe", chosen, value_rows, preferred_element_type=jnp.float32
        )
        new_totals = retained[:, None] * totals + jnp.sum(chosen.astype(jnp.float32), axis=1)
        return ((new_memory, new_totals), (numerator / denominator, denominator, memory, totals))

    final_running, stored = lax.scan(
        advance, initial, (query_blocks, key_blocks, value_blocks, doc_blocks, before_docs)
    )
    return stored


def attend_backward(
    query_blocks,
    key_blocks,
    value_blocks,
    doc_blocks,
    before_docs,
    after_docs,
    stored,
    result_grads,
):
    result_blocks, denominators, memories, totals_before = stored
    sequences = query_blocks.shape[1]
    features = query_blocks.shape[-1]
    initial = (
        jnp.zeros((sequences, features, value_blocks.shape[-1]), jnp.float32),
        jnp.zeros((sequences, features), jnp.float32),
    )

    def retreat(running, pieces):
        later, later_totals = running
        (
            query_rows,
            key_rows,
            value_rows,
            doc_block,
            before_doc,
            after_doc,
            result_rows,
            denominator,
            memory,
            totals,
            result_grad,
        ) = pieces
        query_wide = query_rows.astype(jnp.float32)
        key_wide = key_rows.astype(jnp.float32)
        value_wide = value_rows.astype(jnp.float32)
        allowed = allowed_pairs(doc_block)
        weights = jnp.where(
            allowed,
            jnp.einsum("sbf,scf->sbc", query_rows, key_rows, preferred_element_type=jnp.float32),
            0.0,
        )
        numerator_grad = result_grad / denominator
        denominator_grad = -jnp.sum(result_grad * result_rows, axis=-1, keepdims=True) / denominator
        weight_grad = jnp.where(
            allowed,
            jnp.einsum("sbe,sce->sbc", numerator_grad, value_wide, precision=EXACT)
            + denominator_grad,
            0.0,
        )
        carried = (doc_block == before_doc[:, None]).astype(jnp.float32)[:, :, None]
        query_grad = jnp.einsum(
            "sbc,scf->sbf", weight_grad, key_wide, precision=EXACT
        ) + carried * (
            jnp.einsum("sbe,sfe->sbf", numerator_grad, memory, precision=EXACT)
            + denominator_grad * totals[:, None, :]
        )
        linked = (doc_block == after_doc[:, None]).astype(jnp.float32)[:, :, None]
        key_grad = jnp.einsum("sbc,sbf->scf", weight_grad, query_wide, precision=EXACT) + linked * (
            jnp.einsum("sbe,sfe->sbf", value_wide, later, precision=EXACT)
            + later_totals[:, None, :]
        )
        value_grad = jnp.einsum(
            "sbc,sbe->sce", weights, numerator_grad, precision=EXACT
        ) + linked * jnp.einsum("sbf,sfe->sbe", key_wide, later, precision=EXACT)
        first_doc = doc_block[:, 0]
        retained = (first_doc == after_doc).astype(jnp.float32)
        chosen = query_wide * (doc_block == first_doc[:, None]).astype(jnp.float32)[:, :, None]
        new_later = retained[:, None, None] * later + jnp.einsum(
            "sbf,sbe->sfe", chosen, numerator_grad, precision=EXACT
        )
        new_totals = retained[:, None] * later_totals + jnp.sum(chosen * denominator_grad, axis=1)
        return ((new_later, new_totals), (query_grad, key_grad, value_grad))

    final_running, grads = lax.scan(
        retreat,
        initial,
        (
            query_blocks,
            key_blocks,
            value_blocks,
            doc_blocks,
            before_docs,
            after_docs,
            result_blocks,
            denominators,
            memories,
            totals_before,
            result_grads,
        ),
        reverse=True,
    )
    return grads


def on_device(
    inputs,
    qkv_weight,
    qkv_bias,
    dense_weight,
    up_weight,
    up_bias,
    down_weight,
    out_bias,
    gain_one,
    shift_one,
    gain_two,
    shift_two,
    feature_omega,
    doc_ids,
    out_grad,
):
    local_rows = inputs.astype(jnp.float32)
    model_width = local_rows.shape[1]
    first_gain = gain_one.astype(jnp.float32)
    second_gain = gain_two.astype(jnp.float32)
    norm_values, norm_pull = jax.vjp(
        both_norms,
        local_rows,
        first_gain,
        shift_one.astype(jnp.float32),
        second_gain,
        shift_two.astype(jnp.float32),
    )
    whole_one, whole_two = (
        lax.all_gather(norm_values[0].astype(jnp.bfloat16), "tensor", axis=0, tiled=True),
        lax.all_gather(norm_values[1].astype(jnp.bfloat16), "tensor", axis=0, tiled=True),
    )
    group_rows = whole_one.shape[0]
    sequences = doc_ids.shape[0]
    block_rows = min(512, LEN // 4)
    projected = jnp.dot(
        whole_one, qkv_weight, preferred_element_type=jnp.float32
    ) + qkv_bias.astype(jnp.float32)
    hidden = jnp.dot(whole_two, up_weight, preferred_element_type=jnp.float32) + up_bias.astype(
        jnp.float32
    )
    activated_exact, gelu_pull = jax.vjp(exact_gelu, hidden)
    activated = activated_exact.astype(jnp.bfloat16)
    cosine_table, sine_table = rotary_tables(jnp.arange(group_rows) % LEN, ROT)
    mixing = jnp.dot(dct_matrix(HEAD_DIM), feature_omega, precision=EXACT)
    doc_blocks = to_blocks(doc_ids.reshape(group_rows), sequences, block_rows)
    before_docs = jnp.concatenate(
        [jnp.full((1, sequences), -1, jnp.int32), doc_blocks[:-1, :, -1]], axis=0
    )
    after_docs = jnp.concatenate(
        [doc_blocks[1:, :, 0], jnp.full((1, sequences), -1, jnp.int32)], axis=0
    )

    def features_of(token_rows):
        return feature_map(token_rows, cosine_table, sine_table, mixing)

    local_heads = qkv_weight.shape[1] // (3 * HEAD_DIM)
    head_saved = []
    head_results = []
    for head_index in range(local_heads):
        column_base = head_index * 3 * HEAD_DIM
        query_exact, query_pull = jax.vjp(
            features_of, projected[:, column_base : column_base + HEAD_DIM]
        )
        key_exact, key_pull = jax.vjp(
            features_of, projected[:, column_base + HEAD_DIM : column_base + 2 * HEAD_DIM]
        )
        value_rows = projected[:, column_base + 2 * HEAD_DIM : column_base + 3 * HEAD_DIM].astype(
            jnp.bfloat16
        )
        blocks = (
            to_blocks(query_exact.astype(jnp.bfloat16), sequences, block_rows),
            to_blocks(key_exact.astype(jnp.bfloat16), sequences, block_rows),
            to_blocks(value_rows, sequences, block_rows),
        )
        stored = attend_forward(blocks[0], blocks[1], blocks[2], doc_blocks, before_docs)
        head_results.append(from_blocks(stored[0]))
        head_saved.append((blocks, stored, query_pull, key_pull))
    merged = jnp.concatenate(head_results, axis=1).astype(jnp.bfloat16)
    branch_total = lax.psum_scatter(
        jnp.dot(merged, dense_weight, preferred_element_type=jnp.float32),
        "tensor",
        scatter_dimension=0,
        tiled=True,
    ) + lax.psum_scatter(
        jnp.dot(activated, down_weight, preferred_element_type=jnp.float32).astype(jnp.bfloat16),
        "tensor",
        scatter_dimension=0,
        tiled=True,
    ).astype(
        jnp.float32
    )
    layer_out = (local_rows + branch_total + out_bias.astype(jnp.float32)).astype(jnp.bfloat16)
    grad_whole = lax.all_gather(out_grad, "tensor", axis=0, tiled=True)
    merged_grad = jnp.einsum(
        "td,ed->te", grad_whole, dense_weight, preferred_element_type=jnp.float32
    )
    dense_weight_grad = jnp.einsum(
        "te,td->ed", merged, grad_whole, preferred_element_type=jnp.float32
    )
    down_weight_grad = jnp.einsum(
        "tf,td->fd", activated, grad_whole, preferred_element_type=jnp.float32
    )
    activated_grad = jnp.einsum(
        "td,fd->tf", grad_whole, down_weight, preferred_element_type=jnp.float32
    )
    hidden_grad = gelu_pull(activated_grad)[0].astype(jnp.bfloat16)
    up_weight_grad = jnp.einsum(
        "td,tf->df", whole_two, hidden_grad, preferred_element_type=jnp.float32
    )
    up_bias_grad = jnp.sum(hidden_grad, axis=0, dtype=jnp.float32)
    column_grads = []
    for head_index in range(local_heads):
        blocks, stored, query_pull, key_pull = head_saved[head_index]
        result_grads = to_blocks(
            merged_grad[:, head_index * HEAD_DIM : (head_index + 1) * HEAD_DIM],
            sequences,
            block_rows,
        )
        query_grad, key_grad, value_grad = attend_backward(
            blocks[0],
            blocks[1],
            blocks[2],
            doc_blocks,
            before_docs,
            after_docs,
            stored,
            result_grads,
        )
        column_grads.extend(
            [
                query_pull(from_blocks(query_grad))[0],
                key_pull(from_blocks(key_grad))[0],
                from_blocks(value_grad),
            ]
        )
    qkv_grad = jnp.concatenate(column_grads, axis=1).astype(jnp.bfloat16)
    qkv_weight_grad = jnp.einsum(
        "td,tc->dc", whole_one, qkv_grad, preferred_element_type=jnp.float32
    )
    qkv_bias_grad = jnp.sum(qkv_grad, axis=0, dtype=jnp.float32)
    local_grad = out_grad.astype(jnp.float32)
    norm_grads = lax.psum_scatter(
        jnp.concatenate(
            [
                jnp.einsum("tc,dc->td", qkv_grad, qkv_weight, preferred_element_type=jnp.float32),
                jnp.einsum("tf,df->td", hidden_grad, up_weight, preferred_element_type=jnp.float32),
            ],
            axis=1,
        ),
        "tensor",
        scatter_dimension=0,
        tiled=True,
    )
    row_part, first_gain_grad, first_shift_grad, second_gain_grad, second_shift_grad = norm_pull(
        (norm_grads[:, :model_width], norm_grads[:, model_width:])
    )
    input_grad = local_grad + row_part
    vector_part = lax.psum_scatter(
        jnp.stack(
            [
                first_gain_grad,
                first_shift_grad,
                second_gain_grad,
                second_shift_grad,
                jnp.sum(local_grad, axis=0),
            ]
        ),
        "tensor",
        scatter_dimension=1,
        tiled=True,
    )
    summed = lax.psum(
        (
            qkv_weight_grad,
            qkv_bias_grad,
            dense_weight_grad,
            up_weight_grad,
            up_bias_grad,
            down_weight_grad,
            vector_part,
        ),
        "dp",
    )
    vectors = summed[6]
    return (
        layer_out,
        input_grad,
        summed[0],
        summed[1],
        summed[2],
        summed[3],
        summed[4],
        summed[5],
        vectors[4],
        vectors[0],
        vectors[1],
        vectors[2],
        vectors[3],
    )


def solution(mesh):
    in_specs = (
        P(("dp", "tensor"), None),
        P(None, "tensor"),
        P("tensor"),
        P("tensor", None),
        P(None, "tensor"),
        P("tensor"),
        P("tensor", None),
        P(),
        P(),
        P(),
        P(),
        P(),
        P(),
        P("dp", None),
        P(("dp", "tensor"), None),
    )
    out_specs = (
        P(("dp", "tensor"), None),
        P(("dp", "tensor"), None),
        P(None, "tensor"),
        P("tensor"),
        P("tensor", None),
        P(None, "tensor"),
        P("tensor"),
        P("tensor", None),
        P("tensor"),
        P("tensor"),
        P("tensor"),
        P("tensor"),
        P("tensor"),
    )
    return jax.shard_map(
        on_device, mesh=mesh, in_specs=in_specs, out_specs=out_specs, check_vma=False
    )
```

profile of v0, /device:TPU:0, one launch (start us, length us, event | category | flops | bytes accessed | tf_op | source)
XLA Modules:
  0.0 1256.8 jit_solution(18088975919537195365)
XLA Ops:
  22.2 64.1 %all-gather.8.cloned.1.call-done = bf16[2048,1024]{1,0:T(8,128)(2,1)} async-done(((bf16[256,1024]{1,0:T(8,128)(2,1)}), bf16[2048,1024]{1,0:T(8,128)(2,1)}) %all-gather.8.cloned.1.call-update) | async-done | bytes 4194320 | tf_op jit(solution)/shard_map/all_gather | solution.py:312
  86.4 3.7 fusion.330
  91.8 68.9 %all-gather.4.cloned.1.call-done = bf16[2048,1024]{1,0:T(8,128)(2,1)} async-done(((bf16[256,1024]{1,0:T(8,128)(2,1)}), bf16[2048,1024]{1,0:T(8,128)(2,1)}) %all-gather.4.cloned.1.call-update) | async-done | bytes 4194320 | tf_op jit(solution)/shard_map/all_gather | solution.py:248
  160.7 5.7 fusion.325
  179.6 37.3 %while.89 = (s32[]{:T(128)}, f32[1,64,64]{2,1,0:T(8,128)S(1)}, f32[1,64]{1,0:T(1,128)S(1)}, f32[4,1,512,64]{2,3,1,0:T(8,128)}, f32[4,1,512,1]{2,3,1,0:T(1,128)},...) while((s32[]{:T(128)}, f32[1,64,64]{2,1,0:T(8,128)S(1)}, ...), condition=%wide.region_9.10_spmd.clone, body=%wide.region_6.9_spmd.clone.sunk | while | flops 266197760 | bytes 3668453 | solution.py:117
  218.7 125.6 %while.91 = (s32[]{:T(128)}, f32[1,64,64]{2,1,0:T(8,128)}, f32[1,64]{1,0:T(1,128)}, f32[4,1,512,64]{2,0,3,1:T(4,128)}, f32[4,1,512,64]{2,0,3,1:T(4,128)}, /*inde...) while((s32[]{:T(128)}, f32[1,64,64]{2,1,0:T(8,128)}, ...), condition=%wide.region_19.20_spmd.clone, body=%wide.region_16.19_spmd.clone.sunk | while | flops 942595712 | bytes 11318790 | solution.py:197
  236.9 3.6 dynamic_update_slice.133
  268.5 3.6 dynamic_update_slice.133
  300.1 3.6 dynamic_update_slice.133
  331.6 3.6 dynamic_update_slice.133
  350.8 35.3 %while.88 = (s32[]{:T(128)}, f32[1,64,64]{2,1,0:T(8,128)S(1)}, f32[1,64]{1,0:T(1,128)S(1)}, f32[4,1,512,64]{2,3,1,0:T(8,128)}, f32[4,1,512,1]{2,3,1,0:T(1,128)S(...) while((s32[]{:T(128)}, f32[1,64,64]{2,1,0:T(8,128)S(1)}, ...), condition=%wide.region_5.6_spmd.clone, body=%wide.region_2.5_spmd.clone.sunk | while | flops 266197760 | bytes 3668709 | solution.py:117
  387.8 107.8 %while.90 = (s32[]{:T(128)}, f32[1,64,64]{2,1,0:T(8,128)}, f32[1,64]{1,0:T(1,128)}, f32[4,1,512,64]{2,0,3,1:T(4,128)}, f32[4,1,512,64]{2,0,3,1:T(4,128)}, /*inde...) while((s32[]{:T(128)}, f32[1,64,64]{2,1,0:T(8,128)}, ...), condition=%wide.region_15.16_spmd.clone, body=%wide.region_12.15_spmd.clone.sunk | while | flops 942595712 | bytes 11392122 | solution.py:197
  403.7 3.6 dynamic_update_slice.130
  430.7 3.6 dynamic_update_slice.130
  457.8 3.6 dynamic_update_slice.130
  504.6 5.7 fusion.331
  510.3 5.0 fusion.329
  515.4 13.6 %convert_reduce_fusion.2 = (f32[512]{0:T(512)S(1)}, bf16[2048,512]{1,0:T(8,128)(2,1)S(1)}, f32[2048,512]{1,0:T(8,128)}) fusion(f32[2048,512]{1,0:T(8,128)S(1)} %fusion.329, f32[512]{0:T(512)S(1)} %copy-done.62, bf16[2048,1024]{1,0:T(8,128)(2,1)S(1)} %copy-done.1, bf16[512,1024]{1,0:T(8,128)(2,1)S(1)} %copy-done), kind=kOutput, calls=%fused_computation.269 | convolution fusion | flops 2226126336 | bytes 15732736 | tf_op jit(solution)/shard_map/td,fd->tf/dot_general | solution.py:322
  532.7 6.3 pad_maximum_fusion
  539.1 4.6 multiply_convert_fusion
  545.0 4.3 convolution_convert_fusion
  552.9 4.6 fusion.328
  558.2 5.9 fusion.333
  564.0 3.7 fusion.335
  567.7 3.7 fusion.336
  571.4 248.1 %reduce-scatter.9.cloned.1.call-done = f32[256,2048]{1,0:T(8,128)} async-done(((f32[2048,2048]{1,0:T(8,128)}), f32[256,2048]{1,0:T(8,128)}) %reduce-scatter.9.cloned.1.call-update) | async-done | bytes 2097168 | tf_op jit(solution)/shard_map/reduce_scatter | solution.py:361
  824.5 85.9 %reduce-scatter.7.cloned.1.call-done = bf16[256,1024]{1,0:T(8,128)(2,1)} async-done(((bf16[2048,1024]{1,0:T(8,128)(2,1)}), bf16[256,1024]{1,0:T(8,128)(2,1)}) %reduce-scatter.7.cloned.1.call-update) | async-done | bytes 524304 | tf_op jit(solution)/shard_map/reduce_scatter | solution.py:303
  910.4 152.3 %reduce-scatter.5.cloned.1.call-done = f32[256,1024]{1,0:T(8,128)} async-done(((f32[2048,1024]{1,0:T(8,128)}), f32[256,1024]{1,0:T(8,128)}) %reduce-scatter.5.cloned.1.call-update) | async-done | bytes 1048592 | tf_op jit(solution)/shard_map/reduce_scatter | solution.py:298
  1067.0 3.9 fusion.334
  1072.5 47.0 %reduce-scatter.11.cloned.1.call-done = f32[5,128]{1,0:T(8,128)} async-done(((f32[5,1024]{1,0:T(8,128)}), f32[5,128]{1,0:T(8,128)}) %reduce-scatter.11.cloned.1.call-update) | async-done | bytes 2576 | tf_op jit(solution)/shard_map/reduce_scatter | solution.py:377
  1119.6 6.4 all-reduce.12
  1126.5 115.6 %all-reduce.16.cloned.1.call-done = (f32[1024,384]{1,0:T(8,128)}, f32[128,1024]{1,0:T(8,128)}, f32[1024,512]{1,0:T(8,128)}, f32[512,1024]{1,0:T(8,128)}) async-done(((f32[1024,384]{1,0:T(8,128)}, f32[128,1024]{1,0:T(8,128)}, f32[1024,512]{1,0:T(8,128)}, f32[512,1024]{1,0:T(8,128)}), (f32[1024,384]{1,0:T(8,128)}, f32[128,1024]{1,0:T(8,128)}, f32[1024,512]{1,0:T(8,128)}, ...) | async-done | bytes 6291472 | tf_op jit(solution)/shard_map/psum | solution.py:391
  (721 shorter events, 343.9 us)
Async XLA Ops:
  7.2 508.1 %copy-start = (bf16[512,1024]{1,0:T(8,128)(2,1)S(1)}, bf16[512,1024]{1,0:T(8,128)(2,1)}, u32[]{:S(2)}) copy-start(bf16[512,1024]{1,0:T(8,128)(2,1)} %param.29) | copy-start | bytes 3145732
  7.2 79.1 %copy-start.30 = (bf16[128,1024]{1,0:T(8,128)(2,1)S(1)}, bf16[128,1024]{1,0:T(8,128)(2,1)}, u32[]{:S(2)}) copy-start(bf16[128,1024]{1,0:T(8,128)(2,1)} %param.26) | copy-start | bytes 786436
  7.2 79.1 %all-gather.8.cloned.1.call-start = ((), (), s32[]{:S(2)}) async-start(), calls=%async_computation.8 | async-start | bytes 4718592 | tf_op jit(solution)/shard_map/all_gather | solution.py:312
  8.0 152.7 %all-gather.4.cloned.1.call-start = ((), (), s32[]{:S(2)}) async-start(), calls=%async_computation.4 | async-start | bytes 4718592 | tf_op jit(solution)/shard_map/all_gather | solution.py:248
  8.7 77.6 %copy-start.46 = (f32[1024]{0:T(1024)}, f32[1024]{0:T(1024)S(1)}, u32[]{:S(2)}) copy-start(f32[1024]{0:T(1024)S(1)} %convert_element_type.410) | copy-start | bytes 12292
  9.4 76.9 %copy-start.48 = (f32[1024]{0:T(1024)}, f32[1024]{0:T(1024)S(1)}, u32[]{:S(2)}) copy-start(f32[1024]{0:T(1024)S(1)} %convert_element_type.419) | copy-start | bytes 12292
  12.0 74.4 %copy-start.54 = (f32[256]{0:T(256)}, f32[256]{0:T(256)S(1)}, u32[]{:S(2)}) copy-start(f32[256]{0:T(256)S(1)} %broadcast_multiply_fusion) | copy-start | bytes 3076
  13.3 73.0 %copy-start.60 = (f32[256]{0:T(256)}, f32[256]{0:T(256)S(1)}, u32[]{:S(2)}) copy-start(f32[256]{0:T(256)S(1)} %fusion.206) | copy-start | bytes 3076
  13.3 73.0 %copy-start.58 = (f32[256]{0:T(256)}, f32[256]{0:T(256)S(1)}, u32[]{:S(2)}) copy-start(f32[256]{0:T(256)S(1)} %fusion.304) | copy-start | bytes 3076
  15.7 494.6 %all-gather.6.cloned.1.call-start = ((), (), s32[]{:S(2)}) async-start(), calls=%async_computation.6 | async-start | bytes 4718592 | tf_op jit(solution)/shard_map/all_gather | solution.py:249
  16.5 803.1 %reduce-scatter.9.cloned.1.call-start = ((), (), s32[]{:S(2)}) async-start(), calls=%async_computation.9 | async-start | bytes 18874368 | tf_op jit(solution)/shard_map/reduce_scatter | solution.py:361
  22.2 152.6 %copy-start.15 = (f32[64,64]{1,0:T(8,128)}, f32[64,64]{1,0:T(8,128)S(1)}, u32[]{:S(2)}) copy-start(f32[64,64]{1,0:T(8,128)S(1)} %fusion.291) | copy-start | bytes 49156
  90.1 70.7 %copy-start.33 = (bf16[1024,384]{1,0:T(8,128)(2,1)S(1)}, bf16[1024,384]{1,0:T(8,128)(2,1)}, u32[]{:S(2)}) copy-start(bf16[1024,384]{1,0:T(8,128)(2,1)} %param.24) | copy-start | bytes 2359300
  228.5 15.7 %copy-start.38 = (s32[1,1,512]{2,1,0:T(1,128)S(1)}, s32[1,1,512]{2,1,0:T(1,128)}, u32[]{:S(2)}) copy-start(s32[1,1,512]{2,1,0:T(1,128)} %copy-done.37) | copy-start | bytes 6148 | tf_op jit(solution)/shard_map/while
  259.4 16.4 %copy-start.38 = (s32[1,1,512]{2,1,0:T(1,128)S(1)}, s32[1,1,512]{2,1,0:T(1,128)}, u32[]{:S(2)}) copy-start(s32[1,1,512]{2,1,0:T(1,128)} %copy-done.37) | copy-start | bytes 6148 | tf_op jit(solution)/shard_map/while
  291.0 16.4 %copy-start.38 = (s32[1,1,512]{2,1,0:T(1,128)S(1)}, s32[1,1,512]{2,1,0:T(1,128)}, u32[]{:S(2)}) copy-start(s32[1,1,512]{2,1,0:T(1,128)} %copy-done.37) | copy-start | bytes 6148 | tf_op jit(solution)/shard_map/while
  322.6 16.4 %copy-start.38 = (s32[1,1,512]{2,1,0:T(1,128)S(1)}, s32[1,1,512]{2,1,0:T(1,128)}, u32[]{:S(2)}) copy-start(s32[1,1,512]{2,1,0:T(1,128)} %copy-done.37) | copy-start | bytes 6148 | tf_op jit(solution)/shard_map/while
  450.0 15.1 %copy-start.40 = (s32[1,1,512]{2,1,0:T(1,128)S(1)}, s32[1,1,512]{2,1,0:T(1,128)}, u32[]{:S(2)}) copy-start(s32[1,1,512]{2,1,0:T(1,128)} %copy-done.39) | copy-start | bytes 6148 | tf_op jit(solution)/shard_map/while
  477.1 15.1 %copy-start.40 = (s32[1,1,512]{2,1,0:T(1,128)S(1)}, s32[1,1,512]{2,1,0:T(1,128)}, u32[]{:S(2)}) copy-start(s32[1,1,512]{2,1,0:T(1,128)} %copy-done.39) | copy-start | bytes 6148 | tf_op jit(solution)/shard_map/while
  504.6 53.6 %copy-start.4 = (bf16[2048,384]{0,1:T(8,128)(2,1)}, bf16[2048,384]{0,1:T(8,128)(2,1)S(1)}, u32[]{:S(2)}) copy-start(bf16[2048,384]{0,1:T(8,128)(2,1)S(1)} %constant_dynamic-update-slice_fusion.6) | copy-start | bytes 4718596
  510.3 22.4 %slice-start = ((s8[8388608]{0:T(1024)(128)(4,1)}), s8[4194304]{0:T(1024)(128)(4,1)S(1)}, s32[]{:S(2)}) async-start(s8[8388608]{0:T(1024)(128)(4,1)} %bitcast.597), calls=%async_computation.12 | async-start | bytes 8388608
  515.4 17.3 %slice-start.1 = ((s8[8388608]{0:T(1024)(128)(4,1)}), s8[4194304]{0:T(1024)(128)(4,1)S(1)}, s32[]{:S(2)}) async-start(s8[8388608]{0:T(1024)(128)(4,1)} %bitcast.597), calls=%async_computation.13 | async-start | bytes 8388608
  539.0 371.4 %reduce-scatter.7.cloned.1.call-start = ((), (), s32[]{:S(2)}) async-start(), calls=%async_computation.7 | async-start | bytes 4718592 | tf_op jit(solution)/shard_map/reduce_scatter | solution.py:303
  549.4 513.4 %reduce-scatter.5.cloned.1.call-start = ((), (), s32[]{:S(2)}) async-start(), calls=%async_computation.5 | async-start | bytes 9437184 | tf_op jit(solution)/shard_map/reduce_scatter | solution.py:298
  557.5 562.1 %reduce-scatter.11.cloned.1.call-start = ((), (), s32[]{:S(2)}) async-start(), calls=%async_computation.10 | async-start | bytes 36864 | tf_op jit(solution)/shard_map/reduce_scatter | solution.py:377
  567.7 251.8 %copy-start.47 = (f32[1024]{0:T(1024)S(1)}, f32[1024]{0:T(1024)}, u32[]{:S(2)}) copy-start(f32[1024]{0:T(1024)} %copy-done.46) | copy-start | bytes 12292
  567.7 251.8 %copy-start.49 = (f32[1024]{0:T(1024)S(1)}, f32[1024]{0:T(1024)}, u32[]{:S(2)}) copy-start(f32[1024]{0:T(1024)} %copy-done.48) | copy-start | bytes 12292
  567.7 251.8 %copy-start.55 = (f32[256]{0:T(256)S(1)}, f32[256]{0:T(256)}, u32[]{:S(2)}) copy-start(f32[256]{0:T(256)} %copy-done.54) | copy-start | bytes 3076
  567.7 254.1 %copy-start.61 = (f32[256]{0:T(256)S(1)}, f32[256]{0:T(256)}, u32[]{:S(2)}) copy-start(f32[256]{0:T(256)} %copy-done.60) | copy-start | bytes 3076
  567.7 254.1 %copy-start.59 = (f32[256]{0:T(256)S(1)}, f32[256]{0:T(256)}, u32[]{:S(2)}) copy-start(f32[256]{0:T(256)} %copy-done.58) | copy-start | bytes 3076
  819.5 243.2 %copy-start.3 = (f32[256,2048]{1,0:T(8,128)S(1)}, f32[256,2048]{1,0:T(8,128)}, u32[]{:S(2)}) copy-start(f32[256,2048]{1,0:T(8,128)} %reduce-scatter.9.cloned.1.call-done) | copy-start | bytes 6291460
  1066.9 175.2 %all-reduce.16.cloned.1.call-start = ((), (), s32[]{:S(2)}) async-start(), calls=%async_computation.11 | async-start | bytes 12582912 | tf_op jit(solution)/shard_map/psum | solution.py:391
  (103 other events, 719.4 us)
Sparse Core Ops, SparseCore 0:
  10.2 76.0 all-gather.7
  89.0 71.6 all-gather.3
  163.4 71.6 all-gather.5
  539.1 280.3 reduce-scatter.8
  823.4 86.9 reduce-scatter.6
  913.9 148.7 reduce-scatter.4
  1067.0 52.4 reduce-scatter.10
  1122.9 119.1 all-reduce.15
where the time goes:
time: 1270 us; the launch traced here: 1260 us
  waiting for transfers between devices  783 us (62%)
  matrix products  181 us (14%)
  local copies, waits for them, and re-layouts  143 us (11%)
  other arithmetic  115 us (9%)
  between operations  15.5 us (1%)
  loops' own time  12.9 us (1%)
    reduce_scatter x1, waiting for transfers between devices, on_device(): lax.psum_scatter(jnp.concatenate([jnp.einsum('tc,dc->td', qkv_grad, qkv_w...  248 us
    reduce_scatter x1, waiting for transfers between devices, on_device(): lax.psum_scatter(jnp.dot(merged, dense_weight, preferred_element_type=jnp...  152 us
    psum x1, waiting for transfers between devices, on_device(): lax.psum((qkv_weight_grad, qkv_bias_grad, dense_weight_grad, up_weight_gr...  116 us
    reduce_scatter x1, waiting for transfers between devices, on_device(): lax.psum_scatter(jnp.dot(activated, down_weight, preferred_element_type=j...  85.9 us
    all_gather x1, waiting for transfers between devices, on_device(): lax.all_gather(norm_values[0].astype(jnp.bfloat16), 'tensor', axis=0, til...  68.9 us
    all_gather x1, waiting for transfers between devices, on_device(): grad_whole = lax.all_gather(out_grad, 'tensor', axis=0, tiled=True)  64.1 us
    dynamic_update_slice x40, local copies, waits for them, and re-layouts, attend_forward(): lax.scan(advance, initial, (query_blocks, key_blocks, value_blocks, doc_b...  62.8 us
    reduce_scatter x1, waiting for transfers between devices, on_device(): lax.psum_scatter(jnp.stack([first_gain_grad, first_shift_grad, second_gai...  47 us
  transfers between devices with their start and end apart: 8, of which 7 were waited for; matrix products, arithmetic and copies ran while one was open for 31% of the time, Pallas kernels for 0%

commit v1 on v0

--- a/solution.py
+++ b/solution.py
@@ -309,7 +309,14 @@
         jnp.float32
     )
     layer_out = (local_rows + branch_total + out_bias.astype(jnp.float32)).astype(jnp.bfloat16)
-    grad_whole = lax.all_gather(out_grad, "tensor", axis=0, tiled=True)
+    ring = [out_grad]
+    for hop in range(7):
+        ring.append(lax.ppermute(ring[-1], "tensor", [(dev, (dev + 1) % 8) for dev in range(8)]))
+    grad_whole = jnp.roll(
+        jnp.concatenate(ring[::-1], axis=0),
+        (lax.axis_index("tensor") + 1) * ring[0].shape[0],
+        axis=0,
+    )
     merged_grad = jnp.einsum(
         "td,ed->te", grad_whole, dense_weight, preferred_element_type=jnp.float32
     )

time: 1270 us -> 1330 us (1.047)
  matrix products: 181 us -> 204 us
  waiting for transfers between devices: 783 us -> 803 us
  local copies, waits for them, and re-layouts: 143 us -> 157 us
    ppermute x0 -> x7, waiting for transfers between devices: none -> 151 us  [on_device(): lax.ppermute(ring[-1], 'tensor', [(dev, (dev + 1) % 8) for dev in range(8)])]
    all_gather x1, waiting for transfers between devices: 68.9 us -> 0.02 us  [on_device(): lax.all_gather(norm_values[0].astype(jnp.bfloat16), 'tensor', axis=0, til...]
    all_gather x1 -> x0, waiting for transfers between devices: 64.1 us -> none  [on_device(): grad_whole = lax.all_gather(out_grad, 'tensor', axis=0, tiled=True)]
    unnamed x135 -> x160, local copies, waits for them, and re-layouts: 25.3 us -> 35.2 us
  transfers between devices with their start and end apart: 8 -> 14, of which waited for: 7 -> 12; matrix products, arithmetic and copies ran while one was open for 31% -> 32% of each run, Pallas kernels for 0% -> 0%
where the time goes in v1:
time: 1330 us; the launch traced here: 1320 us
  waiting for transfers between devices  803 us (60%)
  matrix products  204 us (15%)
  local copies, waits for them, and re-layouts  157 us (12%)
  other arithmetic  120 us (9%)
  between operations  15.4 us (1%)
    reduce_scatter x1, waiting for transfers between devices, on_device(): lax.psum_scatter(jnp.concatenate([jnp.einsum('tc,dc->td', qkv_grad, qkv_w...  251 us
    reduce_scatter x1, waiting for transfers between devices, on_device(): lax.psum_scatter(jnp.dot(merged, dense_weight, preferred_element_type=jnp...  152 us
    ppermute x7, waiting for transfers between devices, on_device(): lax.ppermute(ring[-1], 'tensor', [(dev, (dev + 1) % 8) for dev in range(8)])  151 us
    psum x1, waiting for transfers between devices, on_device(): lax.psum((qkv_weight_grad, qkv_bias_grad, dense_weight_grad, up_weight_gr...  116 us
    reduce_scatter x1, waiting for transfers between devices, on_device(): lax.psum_scatter(jnp.dot(activated, down_weight, preferred_element_type=j...  85.9 us
    dynamic_update_slice x40, local copies, waits for them, and re-layouts, attend_forward(): lax.scan(advance, initial, (query_blocks, key_blocks, value_blocks, doc_b...  62.7 us
    reduce_scatter x1, waiting for transfers between devices, on_device(): lax.psum_scatter(jnp.stack([first_gain_grad, first_shift_grad, second_gai...  47.1 us
    unnamed x160, local copies, waits for them, and re-layouts  35.2 us
  transfers between devices with their start and end apart: 14, of which 12 were waited for; matrix products, arithmetic and copies ran while one was open for 32% of the time, Pallas kernels for 0%

profile of v1, /device:TPU:0, one launch (start us, length us, event | category | flops | bytes accessed | tf_op | source)
XLA Modules:
  0.0 1322.5 jit_solution(1625585084735843579)
XLA Ops:
  18.1 17.5 %collective-permute-done = bf16[256,1024]{1,0:T(8,128)(2,1)S(1)} collective-permute-done((bf16[256,1024]{1,0:T(8,128)(2,1)}, bf16[256,1024]{1,0:T(8,128)(2,1)S(1)}, u32[]{:S(2)}, u32[]{:S(2)}) %collective-permute-start) | collective-permute-done | bytes 524320 | tf_op jit(solution)/shard_map/ppermute | solution.py:314
  36.0 25.5 %collective-permute-done.1 = bf16[256,1024]{1,0:T(8,128)(2,1)S(1)} collective-permute-done((bf16[256,1024]{1,0:T(8,128)(2,1)S(1)}, bf16[256,1024]{1,0:T(8,128)(2,1)S(1)}, u32[]{:S(2)}, u32[]{:S(2)}) %collective-permute-start.1) | collective-permute-done | bytes 524320 | tf_op jit(solution)/shard_map/ppermute | solution.py:314
  62.2 26.8 %collective-permute-done.2 = bf16[256,1024]{1,0:T(8,128)(2,1)S(1)} collective-permute-done((bf16[256,1024]{1,0:T(8,128)(2,1)S(1)}, bf16[256,1024]{1,0:T(8,128)(2,1)S(1)}, u32[]{:S(2)}, u32[]{:S(2)}) %collective-permute-start.2) | collective-permute-done | bytes 524320 | tf_op jit(solution)/shard_map/ppermute | solution.py:314
  89.8 26.7 %collective-permute-done.3 = bf16[256,1024]{1,0:T(8,128)(2,1)S(1)} collective-permute-done((bf16[256,1024]{1,0:T(8,128)(2,1)S(1)}, bf16[256,1024]{1,0:T(8,128)(2,1)S(1)}, u32[]{:S(2)}, u32[]{:S(2)}) %collective-permute-start.3) | collective-permute-done | bytes 524320 | tf_op jit(solution)/shard_map/ppermute | solution.py:314
  117.3 16.4 %collective-permute-done.4 = bf16[256,1024]{1,0:T(8,128)(2,1)} collective-permute-done((bf16[256,1024]{1,0:T(8,128)(2,1)S(1)}, bf16[256,1024]{1,0:T(8,128)(2,1)}, u32[]{:S(2)}, u32[]{:S(2)}) %collective-permute-start.4) | collective-permute-done | bytes 524320 | tf_op jit(solution)/shard_map/ppermute | solution.py:314
  138.0 9.6 collective-permute-done.5
  148.0 29.0 %collective-permute-done.6 = bf16[256,1024]{1,0:T(8,128)(2,1)S(1)} collective-permute-done((bf16[256,1024]{1,0:T(8,128)(2,1)}, bf16[256,1024]{1,0:T(8,128)(2,1)S(1)}, u32[]{:S(2)}, u32[]{:S(2)}) %collective-permute-start.6) | collective-permute-done | bytes 524320 | tf_op jit(solution)/shard_map/ppermute | solution.py:314
  188.1 5.9 fusion.339
  207.8 47.1 %while.89 = (s32[]{:T(128)}, f32[1,64,64]{2,1,0:T(8,128)S(1)}, f32[1,64]{1,0:T(1,128)S(1)}, f32[4,1,512,64]{2,3,1,0:T(8,128)}, f32[4,1,512,1]{2,3,1,0:T(1,128)},...) while((s32[]{:T(128)}, f32[1,64,64]{2,1,0:T(8,128)S(1)}, ...), condition=%wide.region_9.10_spmd.clone, body=%wide.region_6.9_spmd.clone.sunk | while | flops 266197760 | bytes 3652069 | solution.py:117
  262.0 42.9 %while.88 = (s32[]{:T(128)}, f32[1,64,64]{2,1,0:T(8,128)S(1)}, f32[1,64]{1,0:T(1,128)S(1)}, f32[4,1,512,64]{2,3,1,0:T(8,128)}, f32[4,1,512,1]{2,3,1,0:T(1,128)S(...) while((s32[]{:T(128)}, f32[1,64,64]{2,1,0:T(8,128)S(1)}, ...), condition=%wide.region_5.6_spmd.clone, body=%wide.region_2.5_spmd.clone.sunk | while | flops 266197760 | bytes 3652325 | solution.py:117
  306.7 136.4 %while.91 = (s32[]{:T(128)}, f32[1,64,64]{2,1,0:T(8,128)}, f32[1,64]{1,0:T(1,128)}, f32[4,1,512,64]{2,0,3,1:T(4,128)}, f32[4,1,512,64]{2,0,3,1:T(4,128)}, /*inde...) while((s32[]{:T(128)}, f32[1,64,64]{2,1,0:T(8,128)}, ...), condition=%wide.region_19.20_spmd.clone, body=%wide.region_16.19_spmd.clone.sunk | while | flops 942595712 | bytes 10778062 | solution.py:197
  325.8 3.6 dynamic_update_slice.133
  360.1 3.6 dynamic_update_slice.133
  394.3 3.6 dynamic_update_slice.133
  444.8 113.4 %while.90 = (s32[]{:T(128)}, f32[1,64,64]{2,1,0:T(8,128)}, f32[1,64]{1,0:T(1,128)}, f32[4,1,512,64]{2,0,3,1:T(4,128)}, f32[4,1,512,64]{2,0,3,1:T(4,128)}, /*inde...) while((s32[]{:T(128)}, f32[1,64,64]{2,1,0:T(8,128)}, ...), condition=%wide.region_15.16_spmd.clone, body=%wide.region_12.15_spmd.clone.sunk | while | flops 942595712 | bytes 11842542 | solution.py:197
  518.9 3.6 dynamic_update_slice.130
  567.2 5.7 fusion.343
  572.9 13.9 %multiply_convert_fusion = (bf16[2048,512]{1,0:T(8,128)(2,1)}, f32[2048,512]{1,0:T(8,128)S(1)}, f32[2048,512]{1,0:T(8,128)S(1)}) fusion(f32[512]{0:T(512)S(1)} %copy-done.66, bf16[2048,1024]{1,0:T(8,128)(2,1)} %all-gather.5.cloned.1.call-done, bf16[1024,512]{1,0:T(8,128)(2,1)S(1)} %copy-done), kind=kOutput, calls=%fused_computation.271 | convolution fusion | flops 2216689664 | bytes 15730688 | tf_op jit(solution)/shard_map/dot_general | solution.py:257
  586.8 6.3 convert_reduce_fusion.2
  597.2 6.3 pad_maximum_fusion
  603.6 6.2 convolution_convert_fusion
  613.5 4.5 fusion.342
  618.7 5.9 fusion.345
  624.6 6.1 fusion.190
  630.7 3.7 fusion.346
  634.4 251.1 %reduce-scatter.9.cloned.1.call-done = f32[256,2048]{1,0:T(8,128)} async-done(((f32[2048,2048]{1,0:T(8,128)}), f32[256,2048]{1,0:T(8,128)}) %reduce-scatter.9.cloned.1.call-update) | async-done | bytes 2097168 | tf_op jit(solution)/shard_map/reduce_scatter | solution.py:368
  890.5 85.9 %reduce-scatter.7.cloned.1.call-done = bf16[256,1024]{1,0:T(8,128)(2,1)} async-done(((bf16[2048,1024]{1,0:T(8,128)(2,1)}), bf16[256,1024]{1,0:T(8,128)(2,1)}) %reduce-scatter.7.cloned.1.call-update) | async-done | bytes 524304 | tf_op jit(solution)/shard_map/reduce_scatter | solution.py:303
  976.4 152.2 %reduce-scatter.5.cloned.1.call-done = f32[256,1024]{1,0:T(8,128)} async-done(((f32[2048,1024]{1,0:T(8,128)}), f32[256,1024]{1,0:T(8,128)}) %reduce-scatter.5.cloned.1.call-update) | async-done | bytes 1048592 | tf_op jit(solution)/shard_map/reduce_scatter | solution.py:298
  1132.9 3.9 fusion.192
  1138.5 47.1 %reduce-scatter.11.cloned.1.call-done = f32[5,128]{1,0:T(8,128)} async-done(((f32[5,1024]{1,0:T(8,128)}), f32[5,128]{1,0:T(8,128)}) %reduce-scatter.11.cloned.1.call-update) | async-done | bytes 2576 | tf_op jit(solution)/shard_map/reduce_scatter | solution.py:384
  1185.6 6.4 all-reduce.12
  1192.5 115.6 %all-reduce.16.cloned.1.call-done = (f32[1024,384]{1,0:T(8,128)}, f32[128,1024]{1,0:T(8,128)}, f32[1024,512]{1,0:T(8,128)}, f32[512,1024]{1,0:T(8,128)}) async-done(((f32[1024,384]{1,0:T(8,128)}, f32[128,1024]{1,0:T(8,128)}, f32[1024,512]{1,0:T(8,128)}, f32[512,1024]{1,0:T(8,128)}), (f32[1024,384]{1,0:T(8,128)}, f32[128,1024]{1,0:T(8,128)}, f32[1024,512]{1,0:T(8,128)}, ...) | async-done | bytes 6291472 | tf_op jit(solution)/shard_map/psum | solution.py:398
  (700 shorter events, 402.3 us)
Async XLA Ops:
  7.2 565.7 %copy-start = (bf16[1024,512]{1,0:T(8,128)(2,1)S(1)}, bf16[1024,512]{1,0:T(8,128)(2,1)}, u32[]{:S(2)}) copy-start(bf16[1024,512]{1,0:T(8,128)(2,1)} %param.27) | copy-start | bytes 3145732
  7.2 127.4 %copy-start.34 = (s32[1,2048]{1,0:T(1,128)S(1)}, s32[1,2048]{1,0:T(1,128)}, u32[]{:S(2)}) copy-start(s32[1,2048]{1,0:T(1,128)} %param.36) | copy-start | bytes 24580
  7.2 130.2 %copy-start.67 = (bf16[512]{0:T(512)(128)(2,1)S(1)}, bf16[512]{0:T(512)(128)(2,1)}, u32[]{:S(2)}) copy-start(bf16[512]{0:T(512)(128)(2,1)} %param.28) | copy-start | bytes 3076
  7.2 130.8 %copy-start.68 = (bf16[384]{0:T(512)(128)(2,1)S(1)}, bf16[384]{0:T(512)(128)(2,1)}, u32[]{:S(2)}) copy-start(bf16[384]{0:T(512)(128)(2,1)} %param.25) | copy-start | bytes 2308
  7.2 140.4 %copy-start.57 = (f32[64,64]{1,0:T(8,128)S(1)}, f32[64,64]{1,0:T(8,128)}, u32[]{:S(2)}) copy-start(f32[64,64]{1,0:T(8,128)} %param.35) | copy-start | bytes 49156
  7.2 180.9 %all-gather.3.cloned.1.call-start = ((), (), s32[]{:S(2)}) async-start(), calls=%async_computation.4 | async-start | bytes 4718592 | tf_op jit(solution)/shard_map/all_gather | solution.py:248
  9.9 170.6 %copy-start.58 = (f32[256]{0:T(256)}, f32[256]{0:T(256)S(1)}, u32[]{:S(2)}) copy-start(f32[256]{0:T(256)S(1)} %fusion.314) | copy-start | bytes 3076
  15.1 557.8 %all-gather.5.cloned.1.call-start = ((), (), s32[]{:S(2)}) async-start(), calls=%async_computation.6 | async-start | bytes 4718592 | tf_op jit(solution)/shard_map/all_gather | solution.py:249
  15.1 20.5 %collective-permute-start = (bf16[256,1024]{1,0:T(8,128)(2,1)}, bf16[256,1024]{1,0:T(8,128)(2,1)S(1)}, u32[]{:S(2)}, u32[]{:S(2)}) collective-permute-start(bf16[256,1024]{1,0:T(8,128)(2,1)} %param.37), channel_id=1, source_target_pairs={{0,1},{1,2},{2,3},{3,4},{4,5},{5,6},{6,7},{7,0},{8,9},{9,10},{10,1... | collective-permute-start | bytes 1572872 | tf_op jit(solution)/shard_map/ppermute | solution.py:314
  35.6 25.8 %collective-permute-start.1 = (bf16[256,1024]{1,0:T(8,128)(2,1)S(1)}, bf16[256,1024]{1,0:T(8,128)(2,1)S(1)}, u32[]{:S(2)}, u32[]{:S(2)}) collective-permute-start(bf16[256,1024]{1,0:T(8,128)(2,1)S(1)} %collective-permute-done), channel_id=1, source_target_pairs={{0,1},{1,2},{2,3},{3,4},{4,5},{5,6},{6,7},{7,0},{8,9},{9,10},{10,1... | collective-permute-start | bytes 1572872 | tf_op jit(solution)/shard_map/ppermute | solution.py:314
  62.2 26.8 %collective-permute-start.2 = (bf16[256,1024]{1,0:T(8,128)(2,1)S(1)}, bf16[256,1024]{1,0:T(8,128)(2,1)S(1)}, u32[]{:S(2)}, u32[]{:S(2)}) collective-permute-start(bf16[256,1024]{1,0:T(8,128)(2,1)S(1)} %collective-permute-done.1), channel_id=1, source_target_pairs={{0,1},{1,2},{2,3},{3,4},{4,5},{5,6},{6,7},{7,0},{8,9},{9,10},{10,1... | collective-permute-start | bytes 1572872 | tf_op jit(solution)/shard_map/ppermute | solution.py:314
  89.8 26.7 %collective-permute-start.3 = (bf16[256,1024]{1,0:T(8,128)(2,1)S(1)}, bf16[256,1024]{1,0:T(8,128)(2,1)S(1)}, u32[]{:S(2)}, u32[]{:S(2)}) collective-permute-start(bf16[256,1024]{1,0:T(8,128)(2,1)S(1)} %collective-permute-done.2), channel_id=1, source_target_pairs={{0,1},{1,2},{2,3},{3,4},{4,5},{5,6},{6,7},{7,0},{8,9},{9,10},{10,1... | collective-permute-start | bytes 1572872 | tf_op jit(solution)/shard_map/ppermute | solution.py:314
  117.3 16.4 %collective-permute-start.4 = (bf16[256,1024]{1,0:T(8,128)(2,1)S(1)}, bf16[256,1024]{1,0:T(8,128)(2,1)}, u32[]{:S(2)}, u32[]{:S(2)}) collective-permute-start(bf16[256,1024]{1,0:T(8,128)(2,1)S(1)} %collective-permute-done.3), channel_id=1, source_target_pairs={{0,1},{1,2},{2,3},{3,4},{4,5},{5,6},{6,7},{7,0},{8,9},{9,10},{10,1... | collective-permute-start | bytes 1572872 | tf_op jit(solution)/shard_map/ppermute | solution.py:314
  133.6 13.9 %collective-permute-start.5 = (bf16[256,1024]{1,0:T(8,128)(2,1)}, bf16[256,1024]{1,0:T(8,128)(2,1)}, u32[]{:S(2)}, u32[]{:S(2)}) collective-permute-start(bf16[256,1024]{1,0:T(8,128)(2,1)} %collective-permute-done.4), channel_id=1, source_target_pairs={{0,1},{1,2},{2,3},{3,4},{4,5},{5,6},{6,7},{7,0},{8,9},{9,10},{10,1... | collective-permute-start | bytes 1572872 | tf_op jit(solution)/shard_map/ppermute | solution.py:314
  133.7 751.8 %reduce-scatter.9.cloned.1.call-start = ((), (), s32[]{:S(2)}) async-start(), calls=%async_computation.8 | async-start | bytes 18874368 | tf_op jit(solution)/shard_map/reduce_scatter | solution.py:368
  147.6 29.4 %collective-permute-start.6 = (bf16[256,1024]{1,0:T(8,128)(2,1)}, bf16[256,1024]{1,0:T(8,128)(2,1)S(1)}, u32[]{:S(2)}, u32[]{:S(2)}) collective-permute-start(bf16[256,1024]{1,0:T(8,128)(2,1)} %collective-permute-done.5), channel_id=1, source_target_pairs={{0,1},{1,2},{2,3},{3,4},{4,5},{5,6},{6,7},{7,0},{8,9},{9,10},{10,1... | collective-permute-start | bytes 1572872 | tf_op jit(solution)/shard_map/ppermute | solution.py:314
  147.6 51.0 %copy-start.62 = (f32[8]{0:T(128)}, f32[8]{0:T(128)S(1)}, u32[]{:S(2)}) copy-start(f32[8]{0:T(128)S(1)} %negate_power_fusion) | copy-start | bytes 100
  147.6 50.9 %copy-start.52 = (f32[2048]{0:T(1024)}, f32[2048]{0:T(1024)S(1)}, u32[]{:S(2)}) copy-start(f32[2048]{0:T(1024)S(1)} %fusion.310) | copy-start | bytes 24580
  148.0 109.7 %copy-start.15 = (f32[64,64]{1,0:T(8,128)}, f32[64,64]{1,0:T(8,128)S(1)}, u32[]{:S(2)}) copy-start(f32[64,64]{1,0:T(8,128)S(1)} %fusion.301) | copy-start | bytes 49156
  207.8 47.1 %copy-start.38 = (f32[2048,8]{0,1:T(8,128)S(1)}, f32[2048,8]{0,1:T(8,128)}, u32[]{:S(2)}) copy-start(f32[2048,8]{0,1:T(8,128)} %get-tuple-element.1292) | copy-start | bytes 196612
  207.8 47.1 %copy-start.39 = (f32[2048,8]{0,1:T(8,128)S(1)}, f32[2048,8]{0,1:T(8,128)}, u32[]{:S(2)}) copy-start(f32[2048,8]{0,1:T(8,128)} %get-tuple-element.1293) | copy-start | bytes 196612
  567.1 51.6 %copy-start.4 = (bf16[2048,384]{0,1:T(8,128)(2,1)}, bf16[2048,384]{0,1:T(8,128)(2,1)S(1)}, u32[]{:S(2)}) copy-start(bf16[2048,384]{0,1:T(8,128)(2,1)S(1)} %constant_dynamic-update-slice_fusion.22) | copy-start | bytes 4718596
  603.5 372.9 %reduce-scatter.7.cloned.1.call-start = ((), (), s32[]{:S(2)}) async-start(), calls=%async_computation.7 | async-start | bytes 4718592 | tf_op jit(solution)/shard_map/reduce_scatter | solution.py:303
  609.8 518.8 %reduce-scatter.5.cloned.1.call-start = ((), (), s32[]{:S(2)}) async-start(), calls=%async_computation.5 | async-start | bytes 9437184 | tf_op jit(solution)/shard_map/reduce_scatter | solution.py:298
  618.1 567.5 %reduce-scatter.11.cloned.1.call-start = ((), (), s32[]{:S(2)}) async-start(), calls=%async_computation.9 | async-start | bytes 36864 | tf_op jit(solution)/shard_map/reduce_scatter | solution.py:384
  630.7 254.8 %copy-start.49 = (f32[1024]{0:T(1024)S(1)}, f32[1024]{0:T(1024)}, u32[]{:S(2)}) copy-start(f32[1024]{0:T(1024)} %copy-done.48) | copy-start | bytes 12292
  630.7 254.8 %copy-start.51 = (f32[1024]{0:T(1024)S(1)}, f32[1024]{0:T(1024)}, u32[]{:S(2)}) copy-start(f32[1024]{0:T(1024)} %copy-done.50) | copy-start | bytes 12292
  630.7 254.8 %copy-start.56 = (f32[256]{0:T(256)S(1)}, f32[256]{0:T(256)}, u32[]{:S(2)}) copy-start(f32[256]{0:T(256)} %copy-done.55) | copy-start | bytes 3076
  630.7 257.1 %copy-start.61 = (f32[256]{0:T(256)S(1)}, f32[256]{0:T(256)}, u32[]{:S(2)}) copy-start(f32[256]{0:T(256)} %copy-done.60) | copy-start | bytes 3076
  630.7 257.1 %copy-start.59 = (f32[256]{0:T(256)S(1)}, f32[256]{0:T(256)}, u32[]{:S(2)}) copy-start(f32[256]{0:T(256)} %copy-done.58) | copy-start | bytes 3076
  885.5 243.1 %copy-start.2 = (f32[256,2048]{1,0:T(8,128)S(1)}, f32[256,2048]{1,0:T(8,128)}, u32[]{:S(2)}) copy-start(f32[256,2048]{1,0:T(8,128)} %reduce-scatter.9.cloned.1.call-done) | copy-start | bytes 6291460
  1132.9 175.2 %all-reduce.16.cloned.1.call-start = ((), (), s32[]{:S(2)}) async-start(), calls=%async_computation.10 | async-start | bytes 12582912 | tf_op jit(solution)/shard_map/psum | solution.py:398
  (86 other events, 760.6 us)
Sparse Core Ops, SparseCore 0:
  15.2 104.7 all-gather.2
  133.8 85.8 all-gather.4
  603.7 281.7 reduce-scatter.8
  889.4 86.9 reduce-scatter.6
  979.9 148.7 reduce-scatter.4
  1133.0 52.5 reduce-scatter.10
  1188.9 119.1 all-reduce.15
